TPU v7x, 256 devices: a whole 4x4x8 slice. The times are simulated.
256 devices in a mesh: qrow: 16 (over x_hi, y, core), dbcol: 16 (over z, x_lo).
Axes of the slice: x: 4 (x_hi: 2, x_lo: 2; x = x_hi * 2 + x_lo), y: 4, z: 8, core: 2. Of those that a mesh axis runs over, the one named last changes fastest.
Arguments:
- query_desc: bfloat16 [8192, 1024], P('qrow', 'dbcol'), may hold values from -0.1875 to 0.1875
- base_desc: bfloat16 [4096, 1024], P('dbcol', 'qrow'), may hold values from -6 to 6
- slopes: int32 [5], replicated, may hold values from -3 to 3, as said below
Outputs:
- seq_score: bfloat16 [8192, 4096], P('qrow', 'dbcol')
- best_score: float32 [8192], P('qrow')
Inputs may be any that keep to these rules, and one draw needn't show every extreme that they name: `slopes`: 5 distinct values that always include -3 and 3.
All inputs are finite; a program needn't handle non-finite values.
Results may differ from a plain program's by a relative error of at most 0.0041.
Values may be sent and summed in bfloat16 or wider, within the bound.
No kernel may reach another device: no remote copies, remote signals or barrier semaphores. Data moves between devices by JAX's collectives and lax.ppermute only.
A program may use at most 64 MiB of HBM per device.

v0:
```python
import math
import jax
import jax.numpy as jnp
from jax import lax
from jax.sharding import PartitionSpec as P

SEQ = 20
WIN = 10
NSLOPE = 5
ROWS_UP = 19
REACH = 57
HALO = 62
spread_floor = 0.5


def with_halo(cells, sides, width):
    for axis, dim in sides:
        count = lax.axis_size(axis)
        ends = count - 1
        head = lax.slice_in_dim(cells, 0, width, axis=dim)
        tail = lax.slice_in_dim(cells, cells.shape[dim] - width, cells.shape[dim], axis=dim)
        cells = jnp.concatenate(
            [
                lax.ppermute(tail, axis, [(i, (i + 1) % count) for i in range(ends)]),
                cells,
                lax.ppermute(head, axis, [((i + 1) % count, i) for i in range(ends)]),
            ],
            axis=dim,
        )
    return cells


def passed_along(x, axis, by):
    peers = lax.axis_size(axis)
    pairs = [(i, i + by) for i in range(peers) if 0 <= i + by < peers]
    return lax.ppermute(x, axis, pairs)


def normalize(similar, valid_cols, valid_rows, out_cols):
    half_win = WIN // 2
    weights = valid_cols.astype(jnp.float32)
    masked = similar * weights[None, :]
    window_sum = masked[:, 0:out_cols]
    window_sq = window_sum * window_sum
    counts = weights[0:out_cols]
    for offset in range(1, WIN):
        column = masked[:, offset : offset + out_cols]
        window_sum = window_sum + column
        window_sq = window_sq + column * column
        counts = counts + weights[offset : offset + out_cols]
    counts = jnp.maximum(counts, 1.0)[None, :]
    window_mean = window_sum / counts
    window_var = window_sq / counts - window_mean * window_mean
    spread = jnp.sqrt(jnp.maximum(window_var, 0.0))
    middle = similar[:, half_win : half_win + out_cols]
    normed = (middle - window_mean) / jnp.maximum(spread, spread_floor)
    keep = (
        weights[half_win : half_win + out_cols][None, :] * valid_rows.astype(jnp.float32)[:, None]
    )
    return (normed * keep).astype(jnp.bfloat16)


def sequence_scores(normed, slopes, tile_rows, tile_cols):
    best_sum = None
    for slope_pos in range(NSLOPE):
        slope_now = slopes[slope_pos]
        running = jnp.zeros((tile_rows, tile_cols), jnp.float32)
        for back_step in range(SEQ):
            row_first = jnp.int32(ROWS_UP - back_step)
            col_first = REACH - slope_now * back_step
            window = lax.dynamic_slice(normed, (row_first, col_first), (tile_rows, tile_cols))
            running = running + window.astype(jnp.float32)
        best_sum = running if best_sum is None else jnp.maximum(best_sum, running)
    return best_sum * (1.0 / math.sqrt(SEQ))


def local(query_desc, base_desc, slopes):
    tile_rows = query_desc.shape[0]
    tile_cols = base_desc.shape[0]
    col_index = lax.axis_index("dbcol")
    total_cols = tile_cols * lax.axis_size("dbcol")
    column_ids = col_index * tile_cols + jnp.arange(tile_cols + 2 * HALO, dtype=jnp.int32) - HALO
    valid_cols = (column_ids >= 0) & (column_ids < total_cols)
    query_full = lax.all_gather(query_desc, "dbcol", axis=1, tiled=True)
    base_full = lax.all_gather(base_desc, "qrow", axis=1, tiled=True)
    similar = lax.dot_general(
        query_full, base_full, (((1,), (1,)), ((), ())), preferred_element_type=jnp.float32
    )
    widened = with_halo(similar, (("dbcol", 1),), HALO)
    own_rows = jnp.ones((tile_rows,), jnp.bool_)
    normed_core = normalize(widened, valid_cols, own_rows, tile_cols + 2 * REACH)
    upper_normed = passed_along(normed_core[tile_rows - ROWS_UP :], "qrow", 1)
    normed = jnp.concatenate([upper_normed, normed_core], 0)
    scores = sequence_scores(normed, slopes, tile_rows, tile_cols)
    best_sum = lax.pmax(jnp.max(scores, axis=1), "dbcol")
    return (scores.astype(jnp.bfloat16), best_sum)


def solution(mesh):
    placed = (P("qrow", "dbcol"), P("dbcol", "qrow"), P())
    return jax.shard_map(
        local,
        mesh=mesh,
        in_specs=placed,
        out_specs=(P("qrow", "dbcol"), P("qrow")),
        check_vma=False,
    )
```

profile of v0, /device:TPU:4, one launch (start us, length us, event | category | flops | bytes accessed | tf_op | source)
XLA Modules:
  0.0 200.3 jit_solution(1408523695805401262)
XLA Ops:
  7.2 0.0 all-gather.2.cloned.1.call-start
  7.2 0.0 copy-start.1
  7.2 0.7 all-gather.2.cloned.1.call-update
  7.9 0.0 copy-done.1
  7.9 0.7 fusion.200
  73.0 0.0 copy-start
  73.1 0.7 copy-done
  73.8 23.3 %all_gather.7 = bf16[256,1024]{0,1:T(8,128)(2,1)S(1)} all-gather(bf16[256,64]{0,1:T(8,128)(2,1)S(1)} %copy-done), channel_id=1, replica_groups=mesh['qrow'=16,'dbcol'=16] {'qrow'}, dimensions={1}, use_global_device_ids=true | all-gather | bytes 557056 | tf_op jit(solution)/shard_map/all_gather | solution.py:85
  97.1 0.0 all-gather.2.cloned.1.call-done
  97.1 1.7 fusion.201
  98.9 4.0 %collective-permute-start = (f32[512,62]{0,1:T(8,128)S(1)}, f32[512,62]{0,1:T(8,128)S(1)}, u32[]{:S(2)}, u32[]{:S(2)}) collective-permute-start(f32[512,62]{0,1:T(8,128)S(1)} %get-tuple-element.8), channel_id=1, source_target_pairs={{0,1},{1,2},{2,3},{3,4},{4,5},{5,6},{6,7},{7,8},{8,9},{9,10},{10,1... | collective-permute-start | bytes 380936 | tf_op jit(solution)/shard_map/ppermute | solution.py:24
  102.8 1.3 collective-permute-start.1
  104.1 0.1 add_maximum_fusion
  104.2 1.9 collective-permute-done
  106.1 4.1 %collective-permute-done.1 = f32[512,62]{0,1:T(8,128)S(1)} collective-permute-done((f32[512,62]{0,1:T(8,128)S(1)}, f32[512,62]{0,1:T(8,128)S(1)}, u32[]{:S(2)}, u32[]{:S(2)}) %collective-permute-start.1) | collective-permute-done | bytes 127008 | tf_op jit(solution)/shard_map/ppermute | solution.py:26
  110.2 0.1 pad_maximum_fusion
  110.3 1.5 fusion.2
  111.8 0.1 slice.130
  111.9 2.1 %collective-permute-start.2 = (bf16[19,370]{0,1:T(8,128)(2,1)S(1)}, bf16[19,370]{0,1:T(8,128)(2,1)S(1)}, u32[]{:S(2)}, u32[]{:S(2)}) collective-permute-start(bf16[19,370]{0,1:T(8,128)(2,1)S(1)} %slice.130), channel_id=1, source_target_pairs={{0,16},{16,32},{32,48},{48,64},{64,80},{80,96},{96,112},{112,128},... | collective-permute-start | bytes 42188 | tf_op jit(solution)/shard_map/ppermute | solution.py:36
  114.8 6.7 %collective-permute-done.2 = bf16[19,370]{0,1:T(8,128)(2,1)S(1)} collective-permute-done((bf16[19,370]{0,1:T(8,128)(2,1)S(1)}, bf16[19,370]{0,1:T(8,128)(2,1)S(1)}, u32[]{:S(2)}, u32[]{:S(2)}) %collective-permute-start.2) | collective-permute-done | bytes 14092 | tf_op jit(solution)/shard_map/ppermute | solution.py:36
  121.5 35.1 %fusion.197 = (f32[512]{0:T(512)S(1)}, bf16[512,256]{0,1:T(8,128)(2,1)S(1)}) fusion(s32[]{:T(128)S(6)} %select_n.379, s32[]{:T(128)S(6)} %select_n.378, s32[]{:T(128)S(6)} %select_n.377, s32[]{:T(128)S(6)} %select_n.376, s32[]{:T(128)S(6)} %select_n.375, s32[]{:T(128)S(6)} %select_n.374, s32[]{:T(128)S(6)} %select_n.373, s32[]{:T(128)S(6)} %select_n.372, ...), kind=kLoop, calls=%fused_computation.326 | loop fusion | flops 63307264 | bytes 1007996 | tf_op jit(solution)/shard_map/reduce_max | solution.py:95
  156.6 0.8 copy.5
  157.4 36.1 %pmax.7 = f32[512]{0:T(512)} all-reduce(f32[512]{0:T(512)S(1)} %get-tuple-element.4), channel_id=1, replica_groups=mesh['qrow'=16,'dbcol'=16] {'dbcol'}, use_global_device_ids=true, to_apply=%region_1.0 | all-reduce | flops 512 | bytes 4096 | tf_op jit(solution)/shard_map/pmax | solution.py:95
  (2 shorter events, 0.0 us)
Async XLA Ops:
  7.2 90.0 %all-gather.2.cloned.1.call-start = ((), (), s32[]{:S(2)}) async-start(), calls=%async_computation | async-start | bytes 1114112 | tf_op jit(solution)/shard_map/all_gather | solution.py:84
  7.2 0.7 copy-start.1
  73.0 0.8 copy-start
  98.9 7.2 %collective-permute-start = (f32[512,62]{0,1:T(8,128)S(1)}, f32[512,62]{0,1:T(8,128)S(1)}, u32[]{:S(2)}, u32[]{:S(2)}) collective-permute-start(f32[512,62]{0,1:T(8,128)S(1)} %get-tuple-element.8), channel_id=1, source_target_pairs={{0,1},{1,2},{2,3},{3,4},{4,5},{5,6},{6,7},{7,8},{8,9},{9,10},{10,1... | collective-permute-start | bytes 380936 | tf_op jit(solution)/shard_map/ppermute | solution.py:24
  102.8 7.4 %collective-permute-start.1 = (f32[512,62]{0,1:T(8,128)S(1)}, f32[512,62]{0,1:T(8,128)S(1)}, u32[]{:S(2)}, u32[]{:S(2)}) collective-permute-start(f32[512,62]{0,1:T(8,128)S(1)} %get-tuple-element.9), channel_id=1, source_target_pairs={{1,0},{2,1},{3,2},{4,3},{5,4},{6,5},{7,6},{8,7},{9,8},{10,9},{11,1... | collective-permute-start | bytes 380936 | tf_op jit(solution)/shard_map/ppermute | solution.py:26
  111.9 9.5 %collective-permute-start.2 = (bf16[19,370]{0,1:T(8,128)(2,1)S(1)}, bf16[19,370]{0,1:T(8,128)(2,1)S(1)}, u32[]{:S(2)}, u32[]{:S(2)}) collective-permute-start(bf16[19,370]{0,1:T(8,128)(2,1)S(1)} %slice.130), channel_id=1, source_target_pairs={{0,16},{16,32},{32,48},{48,64},{64,80},{80,96},{96,112},{112,128},... | collective-permute-start | bytes 42188 | tf_op jit(solution)/shard_map/ppermute | solution.py:36
Sparse Core Ops, SparseCore 0:
  9.8 71.3 all-gather.1
where the time goes:
time: 202 us; the launch traced here: 200 us
  between operations  79.4 us (39%)
  blocking collectives  59.4 us (29%)
  other arithmetic  36.8 us (18%)
  waiting for transfers between devices  13.3 us (7%)
  starting transfers between devices  7.38 us (4%)
  local copies, waits for them, and re-layouts  2.29 us (1%)
    pmax x1, blocking collectives, local(): best_sum = lax.pmax(jnp.max(scores, axis=1), 'dbcol')  36.1 us
    reduce_max x1, other arithmetic, local(): best_sum = lax.pmax(jnp.max(scores, axis=1), 'dbcol')  35.1 us
    all_gather x1, blocking collectives, local(): base_full = lax.all_gather(base_desc, 'qrow', axis=1, tiled=True)  23.3 us
    ppermute x1, waiting for transfers between devices, passed_along(): return lax.ppermute(x, axis, pairs)  6.67 us
    ppermute x1, waiting for transfers between devices, with_halo(): lax.ppermute(head, axis, [((i + 1) % count, i) for i in range(ends)])  4.12 us
  transfers between devices with their start and end apart: 4, of which 3 were waited for; matrix products, arithmetic and copies ran while one was open for 0% of the time, Pallas kernels for 0%

commit v1 on v0

--- a/solution.py
+++ b/solution.py
@@ -82,7 +82,9 @@
     column_ids = col_index * tile_cols + jnp.arange(tile_cols + 2 * HALO, dtype=jnp.int32) - HALO
     valid_cols = (column_ids >= 0) & (column_ids < total_cols)
     query_full = lax.all_gather(query_desc, "dbcol", axis=1, tiled=True)
-    base_full = lax.all_gather(base_desc, "qrow", axis=1, tiled=True)
+    base_full = jnp.concatenate(
+        lax.all_to_all(jnp.stack([base_desc] * lax.axis_size("qrow")), "qrow", 0, 0), axis=1
+    )
     similar = lax.dot_general(
         query_full, base_full, (((1,), (1,)), ((), ())), preferred_element_type=jnp.float32
     )

time: 202 us -> 186 us (0.921)
  blocking collectives: 59.4 us -> 36.5 us
  starting transfers between devices: 7.38 us -> 14.1 us
    all_gather x1 -> x0, blocking collectives: 23.3 us -> none  [local(): base_full = lax.all_gather(base_desc, 'qrow', axis=1, tiled=True)]
    all_to_all x0 -> x1, starting transfers between devices: none -> 7.58 us  [local(): lax.all_to_all(jnp.stack([base_desc] * lax.axis_size('qrow')), 'qrow', 0, 0)]
  transfers between devices with their start and end apart: 4 -> 5, of which waited for: 3 -> 3; matrix products, arithmetic and copies ran while one was open for 0% -> 1% of each run, Pallas kernels for 0% -> 0%
where the time goes in v1:
time: 186 us; the launch traced here: 185 us
  between operations  79.9 us (43%)
  other arithmetic  36.8 us (20%)
  blocking collectives  36.5 us (20%)
  starting transfers between devices  14.1 us (8%)
  waiting for transfers between devices  13.6 us (7%)
  local copies, waits for them, and re-layouts  2.51 us (1%)
    pmax x1, blocking collectives, local(): best_sum = lax.pmax(jnp.max(scores, axis=1), 'dbcol')  36.5 us
    reduce_max x1, other arithmetic, local(): best_sum = lax.pmax(jnp.max(scores, axis=1), 'dbcol')  35.1 us
    all_to_all x1, starting transfers between devices, local(): lax.all_to_all(jnp.stack([base_desc] * lax.axis_size('qrow')), 'qrow', 0, 0)  7.58 us
    ppermute x1, waiting for transfers between devices, passed_along(): return lax.ppermute(x, axis, pairs)  6.67 us
    ppermute x1, waiting for transfers between devices, with_halo(): lax.ppermute(head, axis, [((i + 1) % count, i) for i in range(ends)])  4.57 us
  transfers between devices with their start and end apart: 5, of which 3 were waited for; matrix products, arithmetic and copies ran while one was open for 1% of the time, Pallas kernels for 0%

profile of v1, /device:TPU:4, one launch (start us, length us, event | category | flops | bytes accessed | tf_op | source)
XLA Modules:
  0.0 185.1 jit_solution(6000841861323679485)
XLA Ops:
  7.2 0.0 copy-start
  7.2 0.0 all-gather.2.cloned.1.call-start
  7.2 0.7 all-gather.2.cloned.1.call-update
  7.9 0.0 copy-done
  7.9 0.9 stack.2
  8.8 0.0 copy-start.1
  8.8 7.6 %all-to-all-start = ((bf16[16,256,64]{1,2,0:T(8,128)(2,1)}), bf16[16,256,64]{1,2,0:T(8,128)(2,1)S(1)}, u32[]{:S(2)}, u32[]{:S(2)}) async-start(bf16[16,256,64]{1,2,0:T(8,128)(2,1)} %stack.2), calls=%async_computation | async-start | bytes 1048576 | tf_op jit(solution)/shard_map/all_to_all | solution.py:86
  16.4 0.0 copy-done.1
  16.4 0.7 fusion.200
  82.1 0.0 all-to-all-done
  82.1 0.0 all-gather.2.cloned.1.call-done
  82.1 1.7 fusion.201
  83.9 3.1 %collective-permute-start = (f32[512,62]{0,1:T(8,128)S(1)}, f32[512,62]{0,1:T(8,128)S(1)}, u32[]{:S(2)}, u32[]{:S(2)}) collective-permute-start(f32[512,62]{0,1:T(8,128)S(1)} %get-tuple-element.10), channel_id=1, source_target_pairs={{0,1},{1,2},{2,3},{3,4},{4,5},{5,6},{6,7},{7,8},{8,9},{9,10},{10,1... | collective-permute-start | bytes 380936 | tf_op jit(solution)/shard_map/ppermute | solution.py:24
  87.0 1.3 collective-permute-start.1
  88.3 0.1 add_maximum_fusion
  88.4 1.6 collective-permute-done
  90.0 4.6 %collective-permute-done.1 = f32[512,62]{0,1:T(8,128)S(1)} collective-permute-done((f32[512,62]{0,1:T(8,128)S(1)}, f32[512,62]{0,1:T(8,128)S(1)}, u32[]{:S(2)}, u32[]{:S(2)}) %collective-permute-start.1) | collective-permute-done | bytes 127008 | tf_op jit(solution)/shard_map/ppermute | solution.py:26
  94.5 0.1 pad_maximum_fusion
  94.7 1.5 fusion.2
  96.2 0.1 slice.130
  96.3 2.1 %collective-permute-start.2 = (bf16[19,370]{0,1:T(8,128)(2,1)S(1)}, bf16[19,370]{0,1:T(8,128)(2,1)S(1)}, u32[]{:S(2)}, u32[]{:S(2)}) collective-permute-start(bf16[19,370]{0,1:T(8,128)(2,1)S(1)} %slice.130), channel_id=1, source_target_pairs={{0,16},{16,32},{32,48},{48,64},{64,80},{80,96},{96,112},{112,128},... | collective-permute-start | bytes 42188 | tf_op jit(solution)/shard_map/ppermute | solution.py:36
  99.2 6.7 %collective-permute-done.2 = bf16[19,370]{0,1:T(8,128)(2,1)S(1)} collective-permute-done((bf16[19,370]{0,1:T(8,128)(2,1)S(1)}, bf16[19,370]{0,1:T(8,128)(2,1)S(1)}, u32[]{:S(2)}, u32[]{:S(2)}) %collective-permute-start.2) | collective-permute-done | bytes 14092 | tf_op jit(solution)/shard_map/ppermute | solution.py:36
  105.8 35.1 %fusion.197 = (f32[512]{0:T(512)S(1)}, bf16[512,256]{0,1:T(8,128)(2,1)S(1)}) fusion(s32[]{:T(128)S(6)} %select_n.379, s32[]{:T(128)S(6)} %select_n.378, s32[]{:T(128)S(6)} %select_n.377, s32[]{:T(128)S(6)} %select_n.376, s32[]{:T(128)S(6)} %select_n.375, s32[]{:T(128)S(6)} %select_n.374, s32[]{:T(128)S(6)} %select_n.373, s32[]{:T(128)S(6)} %select_n.372, ...), kind=kLoop, calls=%fused_computation.326 | loop fusion | flops 63307264 | bytes 1007996 | tf_op jit(solution)/shard_map/reduce_max | solution.py:97
  140.9 0.8 copy.7
  141.7 36.5 %pmax.7 = f32[512]{0:T(512)} all-reduce(f32[512]{0:T(512)S(1)} %get-tuple-element.6), channel_id=1, replica_groups=mesh['qrow'=16,'dbcol'=16] {'dbcol'}, use_global_device_ids=true, to_apply=%region_1.0 | all-reduce | flops 512 | bytes 4096 | tf_op jit(solution)/shard_map/pmax | solution.py:97
  (2 shorter events, 0.0 us)
Async XLA Ops:
  7.2 0.8 copy-start
  7.2 74.9 %all-gather.2.cloned.1.call-start = ((), (), s32[]{:S(2)}) async-start(), calls=%async_computation.1 | async-start | bytes 1114112 | tf_op jit(solution)/shard_map/all_gather | solution.py:84
  8.8 7.6 %copy-start.1 = (s32[5]{0:T(128)S(1)}, s32[5]{0:T(128)}, u32[]{:S(2)}) copy-start(s32[5]{0:T(128)} %param.5) | copy-start | bytes 64
  8.8 73.3 %all-to-all-start = ((bf16[16,256,64]{1,2,0:T(8,128)(2,1)}), bf16[16,256,64]{1,2,0:T(8,128)(2,1)S(1)}, u32[]{:S(2)}, u32[]{:S(2)}) async-start(bf16[16,256,64]{1,2,0:T(8,128)(2,1)} %stack.2), calls=%async_computation | async-start | bytes 1048576 | tf_op jit(solution)/shard_map/all_to_all | solution.py:86
  83.9 6.1 %collective-permute-start = (f32[512,62]{0,1:T(8,128)S(1)}, f32[512,62]{0,1:T(8,128)S(1)}, u32[]{:S(2)}, u32[]{:S(2)}) collective-permute-start(f32[512,62]{0,1:T(8,128)S(1)} %get-tuple-element.10), channel_id=1, source_target_pairs={{0,1},{1,2},{2,3},{3,4},{4,5},{5,6},{6,7},{7,8},{8,9},{9,10},{10,1... | collective-permute-start | bytes 380936 | tf_op jit(solution)/shard_map/ppermute | solution.py:24
  87.0 7.6 %collective-permute-start.1 = (f32[512,62]{0,1:T(8,128)S(1)}, f32[512,62]{0,1:T(8,128)S(1)}, u32[]{:S(2)}, u32[]{:S(2)}) collective-permute-start(f32[512,62]{0,1:T(8,128)S(1)} %get-tuple-element.11), channel_id=1, source_target_pairs={{1,0},{2,1},{3,2},{4,3},{5,4},{6,5},{7,6},{8,7},{9,8},{10,9},{11,1... | collective-permute-start | bytes 380936 | tf_op jit(solution)/shard_map/ppermute | solution.py:26
  96.3 9.5 %collective-permute-start.2 = (bf16[19,370]{0,1:T(8,128)(2,1)S(1)}, bf16[19,370]{0,1:T(8,128)(2,1)S(1)}, u32[]{:S(2)}, u32[]{:S(2)}) collective-permute-start(bf16[19,370]{0,1:T(8,128)(2,1)S(1)} %slice.130), channel_id=1, source_target_pairs={{0,16},{16,32},{32,48},{48,64},{64,80},{80,96},{96,112},{112,128},... | collective-permute-start | bytes 42188 | tf_op jit(solution)/shard_map/ppermute | solution.py:36
Sparse Core Ops, SparseCore 0:
  9.8 71.3 all-gather.1
